TPU v7x, 32 devices: a whole 2x2x4 slice. The times are simulated.
32 devices in a mesh: node: 16 (over z, y, core), local: 2 (over x).
Axes of the slice: x: 2, y: 2, z: 4, core: 2. Of those that a mesh axis runs over, the one named last changes fastest.
Arguments:
- activations: bfloat16 [4096, 4096], P(('node', 'local')), may hold values from -6 to 6
- out_grads: bfloat16 [4096, 512], P(('node', 'local')), may hold values from -6 to 6
- master: float32 [4096, 512], P(('node', 'local')), may hold values from -0.15 to 0.15
- first_moment: float32 [4096, 512], P(('node', 'local')), may hold values from -0.6 to 0.6
- second_moment: float32 [4096, 512], P(('node', 'local')), may hold values from 0.01 to 1
Outputs:
- new_weight: bfloat16 [4096, 512], P('node')
- new_first: float32 [4096, 512], P(('node', 'local'))
- new_second: float32 [4096, 512], P(('node', 'local'))
All inputs are finite; a program needn't handle non-finite values.
Results may differ from a plain program's by a relative error of at most 0.009.
Values may be sent and summed in bfloat16 or wider, within the bound.
No kernel may reach another device: no remote copies, remote signals or barrier semaphores. Data moves between devices by JAX's collectives and lax.ppermute only.
A program may use at most 128 MiB of HBM per device.

v0:
```python
import functools

import jax
import jax.numpy as jnp
from jax import lax
from jax.experimental import pallas as pl
from jax.experimental.pallas import tpu as pltpu
from jax.sharding import PartitionSpec as P


def partner(index, step, count):
    if count & (count - 1) == 0:
        return index ^ step
    return (index + step) % count


class Layout:
    def __init__(self, node_count, local_count):
        self.core = 2 if node_count % 2 == 0 else 1
        rest = node_count // self.core
        self.middle = 2 if rest % 2 == 0 else 1
        self.outer = rest // self.middle
        if self.outer & (self.outer - 1):
            self.middle, self.outer = rest, 1
        self.local = local_count
        self.group = self.middle * self.local

    def split(self, device):
        node, local = device // self.local, device % self.local
        core, rest = node % self.core, node // self.core
        return rest // self.middle, rest % self.middle, core, local

    def join(self, outer, middle, core, local):
        return ((outer * self.middle + middle) * self.core + core) * self.local + local

    def move(self, device, outer=0, group=0, core=0):
        o, m, c, l = self.split(device)
        return self.join(
            partner(o, outer, self.outer),
            partner(m, group // self.local, self.middle),
            partner(c, core, self.core),
            partner(l, group % self.local, self.local),
        )

    def permute(self, value, **steps):
        count = self.outer * self.middle * self.core * self.local
        pairs = [(d, self.move(d, **steps)) for d in range(count)]
        return lax.ppermute(value, ("node", "local"), pairs)

    def peers(self):
        both = [(g // self.local, g % self.local) for g in range(1, self.group)]
        both.sort(key=lambda ml: (ml[0] > 0 and ml[1] > 0, ml[1] > 0))
        return tuple(m * self.local + l for m, l in both)

    def me(self):
        return lax.axis_index("node") * self.local + lax.axis_index("local")


def in_vmem(value):
    return pltpu.with_memory_space_constraint(value, pltpu.VMEM)


SMALL = pltpu.CompilerParams(vmem_limit_bytes=16 * 2**20)


def take_kernel(grid, wanted, rows, activations, *refs):
    *outs, source, sem = refs
    load = pltpu.make_async_copy(activations, source, sem)
    load.start()
    load.wait()
    me = grid.me()
    for (group, steps), out in zip(wanted, outs):
        for j, (o, c) in enumerate((o, c) for c in range(grid.core) for o in steps):
            block = grid.move(me, outer=o, group=group, core=c)
            columns = pl.ds(pl.multiple_of(block * rows, rows), rows)
            out[:, pl.ds(j * rows, rows)] = source[:, columns]


def take(grid, wanted, rows, activations):
    tokens = activations.shape[0]
    if rows % 128:
        me = grid.me()
        out = []
        for group, steps in wanted:
            blocks = [
                grid.move(me, outer=o, group=group, core=c) for c in range(grid.core) for o in steps
            ]
            parts = [lax.dynamic_slice_in_dim(activations, b * rows, rows, 1) for b in blocks]
            out.append(jnp.concatenate(parts, 1))
        return out
    return pl.pallas_call(
        functools.partial(take_kernel, grid, wanted, rows),
        out_shape=[
            pltpu.VMEM((tokens, len(steps) * grid.core * rows), activations.dtype)
            for _, steps in wanted
        ],
        in_specs=[pl.BlockSpec(memory_space=pltpu.HBM)],
        out_specs=[pl.BlockSpec(memory_space=pltpu.VMEM)] * len(wanted),
        scratch_shapes=[
            pltpu.VMEM(activations.shape, activations.dtype),
            pltpu.SemaphoreType.DMA(()),
        ],
        compiler_params=SMALL,
        name="take",
    )(pltpu.with_memory_space_constraint(activations, pltpu.HBM))


def product(left, right):
    return lax.dot_general(
        left, right, (((0,), (0,)), ((), ())), preferred_element_type=jnp.float32
    )


def sums_kernel(members, cores, size, *refs):
    rights, lefts, out = refs[:members], refs[members:-1], refs[-1]
    width = out.shape[-1]
    for j, core in enumerate(cores):
        rows = pl.ds(core * size, size)
        for half in range(2):
            total = None
            for left, right in zip(lefts, rights):
                part = product(left[:, rows], right[:, pl.ds(half * width, width)])
                total = part if total is None else total + part
            out[j, half] = total.astype(out.dtype)


def group_sums(grid, rows, cores, dtype, rights, lefts):
    size, width = lefts[0].shape[1] // grid.core, rights[0].shape[1] // 2
    if rows % 128:
        left = jnp.concatenate(lefts, 0).reshape(-1, grid.core, size)
        right = jnp.concatenate(rights, 0)
        total = [product(left[:, core], right).astype(dtype) for core in cores]
        return jnp.stack([jnp.stack(jnp.split(t, 2, axis=1)) for t in total])
    vmem = pl.BlockSpec(memory_space=pltpu.VMEM)
    operands = (*rights, *lefts)
    return pl.pallas_call(
        functools.partial(sums_kernel, len(rights), cores, size),
        out_shape=pltpu.VMEM((len(cores), 2, size, width), dtype),
        in_specs=[vmem] * len(operands),
        out_specs=vmem,
        compiler_params=SMALL,
        name="sums",
    )(*(in_vmem(v) for v in operands))


def merge_kernel(pieces, kept, *refs):
    got, outs = refs[: -len(pieces)], refs[-len(pieces) :]
    for (start, size, dtype), out in zip(pieces, outs):
        at = pl.ds(start, size)
        for half in range(2):
            total = kept[half, at, :]
            for part in got:
                total += part[half, at, :].astype(jnp.float32)
            out[half] = total.astype(dtype)


def merge(kept, got, pieces):
    _, size, width = kept.shape
    if size % 128:
        total = kept + sum([g.astype(jnp.float32) for g in got])
        return [total[:, start : start + size].astype(dtype) for start, size, dtype in pieces]
    vmem = pl.BlockSpec(memory_space=pltpu.VMEM)
    return pl.pallas_call(
        functools.partial(merge_kernel, pieces),
        out_shape=[pltpu.VMEM((2, size, width), dtype) for _, size, dtype in pieces],
        in_specs=[vmem] * (1 + len(got)),
        out_specs=[vmem] * len(pieces),
        compiler_params=SMALL,
        name="merge",
    )(*(in_vmem(v) for v in (kept, *got)))


def adam(grad, master, first_moment, second_moment):
    new_first = 0.9 * first_moment + 0.1 * grad
    new_second = 0.95 * second_moment + 0.05 * grad * grad
    update = new_first / (1.0 - 0.9**10) / (jnp.sqrt(new_second / (1.0 - 0.95**10)) + 1e-08)
    return (master - 0.01 * update).astype(jnp.bfloat16), new_first, new_second


def update_kernel(count, parts, halves, weights, *refs):
    master, first_moment, second_moment = refs[:3]
    outs = refs[3 + parts * len(halves) :]
    width = master.shape[1] // 2
    for i, half in enumerate(halves):
        total = None
        for part in refs[3 + i * parts : 3 + (i + 1) * parts]:
            part = part[half] if len(part.shape) == 3 else part[...]
            total = part if total is None else total + part.astype(jnp.float32)
        at = pl.ds(half * width, width)
        step = adam(total / count, master[:, at], first_moment[:, at], second_moment[:, at])
        if weights:
            outs[0][...] = step[0]
        else:
            outs[0][:, at] = step[1]
            outs[1][:, at] = step[2]


def update(count, parts, halves, weights, state):
    vmem = pl.BlockSpec(memory_space=pltpu.VMEM)
    rows, cols = state[0].shape
    width = cols // 2
    if rows % 128:
        out = []
        for half, arrived in zip(halves, parts):
            total = sum([(a[half] if a.ndim == 3 else a).astype(jnp.float32) for a in arrived])
            at = slice(half * width, (half + 1) * width)
            out.append(adam(total / count, *(v[:, at] for v in state)))
        if weights:
            return [out[0][0]]
        return [jnp.concatenate([o[i] for o in out], 1) for i in (1, 2)]
    operands = [*state, *(v for part in parts for v in part)]
    if weights:
        out_shape = [pltpu.VMEM((rows, width), jnp.bfloat16)]
    else:
        out_shape = [pltpu.VMEM((rows, cols), jnp.float32)] * 2
    return pl.pallas_call(
        functools.partial(update_kernel, count, len(parts[0]), halves, weights),
        out_shape=out_shape,
        in_specs=[vmem] * len(operands),
        out_specs=[vmem] * len(out_shape),
        compiler_params=SMALL,
        name="adam",
    )(*(in_vmem(v) for v in operands))


def join_kernel(*refs):
    *parts, out, sems = refs
    rows, width = parts[0].shape
    mine = lax.axis_index("local")
    copies = []
    for i, part in enumerate(parts):
        row = (mine if i < 2 else 1 - mine) * rows
        copies.append(
            pltpu.make_async_copy(
                part, out.at[pl.ds(row, rows), pl.ds((i % 2) * width, width)], sems.at[i]
            )
        )
    for copy in copies:
        copy.start()
    for copy in copies:
        copy.wait()


def joined(grid, own):
    rows, width = own[0].shape
    if grid.local != 2 or rows % 128:
        return lax.all_gather(jnp.concatenate(own, 1), "local", axis=0, tiled=True)
    other = []
    for half in own:
        other.append(grid.permute(half, group=1))
    vmem = pl.BlockSpec(memory_space=pltpu.VMEM)
    return pl.pallas_call(
        join_kernel,
        out_shape=jax.ShapeDtypeStruct((2 * rows, 2 * width), own[0].dtype),
        in_specs=[vmem] * 4,
        out_specs=pl.BlockSpec(memory_space=pl.ANY),
        scratch_shapes=[pltpu.SemaphoreType.DMA((4,))],
        compiler_params=SMALL,
        name="join",
    )(*(in_vmem(v) for v in (*own, *other)))


def step(activations, out_grads, *state):
    grid = Layout(lax.axis_size("node"), lax.axis_size("local"))
    rows = state[0].shape[0]
    count = grid.outer * grid.middle * grid.core * grid.local
    groups = grid.peers()
    odd, even = tuple(range(3, grid.outer, 2)), tuple(range(2, grid.outer, 2))
    near = tuple(range(1, min(2, grid.outer)))

    def send(messages):
        out = []
        for g, message in zip(groups, messages):
            out.append(grid.permute(message, group=g))
        return out

    rights = [out_grads] + send([out_grads] * len(groups))
    plan = {"a": odd, "b": even + near, "c": (0,)}
    plan = {name: steps for name, steps in plan.items() if steps}
    peers = (*groups, 0)
    taken = take(grid, [(g, steps) for steps in plan.values() for g in peers], rows, activations)
    lefts = {}
    for j, name in enumerate(plan):
        *messages, own = taken[j * len(peers) : (j + 1) * len(peers)]
        lefts[name] = [own] + send(messages)

    half, full = jnp.bfloat16, jnp.float32

    def sums(name):
        got = []
        if grid.core > 1:
            others = tuple(range(1, grid.core))
            sent = group_sums(grid, rows, others, half, rights, lefts[name])
            got = [grid.permute(sent[c - 1], core=c) for c in others]
        kept = group_sums(grid, rows, (0,), full, rights, lefts[name])[0]
        return kept, got

    def hop(part, outer):
        return grid.permute(part.astype(half), outer=outer)

    split = len(even) * rows
    hops = [[], []]
    if odd:
        (part,) = merge(*sums("a"), [(0, split, half)])
        passed = hop(part, 1)
    if near:
        pieces = [(split, rows, half)] + ([(0, split, full)] if odd else [])
        part, *base = merge(*sums("b"), pieces)
        near_hop = hop(part, 1)
        for h in range(2):
            hops[h].append(near_hop)
    if odd:
        for h in range(2):
            part = base[0][h] + passed[h].astype(full)
            for i, o in enumerate(even):
                hops[h].append(hop(part[i * rows : (i + 1) * rows], o))
    kept, got = sums("c")

    totals = [[kept, *got, *hops[h]] for h in range(2)]
    weights = []
    for h in range(2):
        weights += update(count, totals[h : h + 1], [h], True, state)
    new_first, new_second = update(count, totals, [0, 1], False, state)
    new_weight = joined(grid, weights)
    return (new_weight, new_first, new_second)


def solution(mesh):
    spec = P(("node", "local"), None)
    return jax.shard_map(
        step,
        mesh=mesh,
        in_specs=(spec,) * 5,
        out_specs=(P("node", None), spec, spec),
        check_vma=False,
    )
```

profile of v0, /device:TPU:0, one launch (start us, length us, event | category | flops | bytes accessed | tf_op | source)
XLA Modules:
  0.0 49.8 jit_solution(9882090402351841837)
XLA Ops:
  0.6 3.1 %collective-permute-start = (bf16[128,512]{1,0:T(8,128)(2,1)}, bf16[128,512]{1,0:T(8,128)(2,1)S(1)}, u32[]{:S(2)}, u32[]{:S(2)}) collective-permute-start(bf16[128,512]{1,0:T(8,128)(2,1)} %refs_0_.14), channel_id=1, source_target_pairs={{0,4},{1,5},{2,6},{3,7},{4,0},{5,1},{6,2},{7,3},{8,12},{9,13},{10,... | collective-permute-start | bytes 393224 | tf_op jit(solution)/shard_map/ppermute | solution.py:48
  3.7 1.5 %collective-permute-start.1 = (bf16[128,512]{1,0:T(8,128)(2,1)}, bf16[128,512]{1,0:T(8,128)(2,1)S(1)}, u32[]{:S(2)}, u32[]{:S(2)}) collective-permute-start(bf16[128,512]{1,0:T(8,128)(2,1)} %refs_0_.14), channel_id=1, source_target_pairs={{0,1},{1,0},{2,3},{3,2},{4,5},{5,4},{6,7},{7,6},{8,9},{9,8},{10,11... | collective-permute-start | bytes 393224 | tf_op jit(solution)/shard_map/ppermute | solution.py:48
  5.2 1.5 %take.1 = (bf16[128,256]{1,0:T(8,128)(2,1)S(1)}, bf16[128,256]{1,0:T(8,128)(2,1)S(1)}, bf16[128,256]{1,0:T(8,128)(2,1)S(1)}, bf16[128,256]{1,0:T(8,128)(2,1)S(1)...) custom-call(bf16[128,4096]{1,0:T(8,128)(2,1)} %activations.1), custom_call_target="tpu_custom_call" | custom-call | tf_op jit(solution)/shard_map/take/pallas_call | solution.py:91
  6.8 2.0 %collective-permute-start.7 = (bf16[128,512]{1,0:T(8,128)(2,1)S(1)}, bf16[128,512]{1,0:T(8,128)(2,1)S(1)}, u32[]{:S(2)}, u32[]{:S(2)}) collective-permute-start(bf16[128,512]{1,0:T(8,128)(2,1)S(1)} %get-tuple-element.24), channel_id=1, source_target_pairs={{0,4},{1,5},{2,6},{3,7},{4,0},{5,1},{6,2},{7,3},{8,12},{9,13},{10,... | collective-permute-start | bytes 393224 | tf_op jit(solution)/shard_map/ppermute | solution.py:48
  8.8 1.5 %collective-permute-start.8 = (bf16[128,512]{1,0:T(8,128)(2,1)S(1)}, bf16[128,512]{1,0:T(8,128)(2,1)S(1)}, u32[]{:S(2)}, u32[]{:S(2)}) collective-permute-start(bf16[128,512]{1,0:T(8,128)(2,1)S(1)} %get-tuple-element.25), channel_id=1, source_target_pairs={{0,1},{1,0},{2,3},{3,2},{4,5},{5,4},{6,7},{7,6},{8,9},{9,8},{10,11... | collective-permute-start | bytes 393224 | tf_op jit(solution)/shard_map/ppermute | solution.py:48
  10.3 1.9 %collective-permute-start.12 = (bf16[128,256]{1,0:T(8,128)(2,1)S(1)}, bf16[128,256]{1,0:T(8,128)(2,1)S(1)}, u32[]{:S(2)}, u32[]{:S(2)}) collective-permute-start(bf16[128,256]{1,0:T(8,128)(2,1)S(1)} %get-tuple-element.30), channel_id=1, source_target_pairs={{0,4},{1,5},{2,6},{3,7},{4,0},{5,1},{6,2},{7,3},{8,12},{9,13},{10,... | collective-permute-start | bytes 196616 | tf_op jit(solution)/shard_map/ppermute | solution.py:48
  12.3 0.5 collective-permute-done.2.refs_3_
  12.7 1.8 %collective-permute-start.13 = (bf16[128,256]{1,0:T(8,128)(2,1)S(1)}, bf16[128,256]{1,0:T(8,128)(2,1)S(1)}, u32[]{:S(2)}, u32[]{:S(2)}) collective-permute-start(bf16[128,256]{1,0:T(8,128)(2,1)S(1)} %get-tuple-element.31), channel_id=1, source_target_pairs={{0,1},{1,0},{2,3},{3,2},{4,5},{5,4},{6,7},{7,6},{8,9},{9,8},{10,11... | collective-permute-start | bytes 196616 | tf_op jit(solution)/shard_map/ppermute | solution.py:48
  14.5 1.5 %collective-permute-done.7.refs_5_ = bf16[128,512]{1,0:T(8,128)(2,1)S(1)} collective-permute-done((bf16[128,512]{1,0:T(8,128)(2,1)S(1)}, bf16[128,512]{1,0:T(8,128)(2,1)S(1)}, u32[]{:S(2)}, u32[]{:S(2)}) %collective-permute-start.7) | collective-permute-done | bytes 131104 | tf_op jit(solution)/shard_map/ppermute | solution.py:48
  16.0 2.3 %collective-permute-start.14 = (bf16[128,256]{1,0:T(8,128)(2,1)S(1)}, bf16[128,256]{1,0:T(8,128)(2,1)S(1)}, u32[]{:S(2)}, u32[]{:S(2)}) collective-permute-start(bf16[128,256]{1,0:T(8,128)(2,1)S(1)} %get-tuple-element.32), channel_id=1, source_target_pairs={{0,5},{1,4},{2,7},{3,6},{4,1},{5,0},{6,3},{7,2},{8,13},{9,12},{10,... | collective-permute-start | bytes 196616 | tf_op jit(solution)/shard_map/ppermute | solution.py:48
  18.3 0.5 sums.9
  18.9 0.5 %collective-permute-done.13.refs_6_ = bf16[128,256]{1,0:T(8,128)(2,1)S(1)} collective-permute-done((bf16[128,256]{1,0:T(8,128)(2,1)S(1)}, bf16[128,256]{1,0:T(8,128)(2,1)S(1)}, u32[]{:S(2)}, u32[]{:S(2)}) %collective-permute-start.13) | collective-permute-done | bytes 65568 | tf_op jit(solution)/shard_map/ppermute | solution.py:48
  19.4 1.8 %collective-permute-done.14.refs_7_ = bf16[128,256]{1,0:T(8,128)(2,1)S(1)} collective-permute-done((bf16[128,256]{1,0:T(8,128)(2,1)S(1)}, bf16[128,256]{1,0:T(8,128)(2,1)S(1)}, u32[]{:S(2)}, u32[]{:S(2)}) %collective-permute-start.14) | collective-permute-done | bytes 65568 | tf_op jit(solution)/shard_map/ppermute | solution.py:48
  21.9 1.0 %collective-permute-done.15.refs_0_ = bf16[2,128,256]{2,1,0:T(8,128)(2,1)S(1)} collective-permute-done((bf16[2,128,256]{2,1,0:T(8,128)(2,1)S(1)}, bf16[2,128,256]{2,1,0:T(8,128)(2,1)S(1)}, u32[]{:S(2)}, u32[]{:S(2)}) %collective-permute-start.15) | collective-permute-done | bytes 131104 | tf_op jit(solution)/shard_map/ppermute | solution.py:48
  23.0 1.2 %collective-permute-start.16 = (bf16[2,128,256]{2,1,0:T(8,128)(2,1)S(1)}, bf16[2,128,256]{2,1,0:T(8,128)(2,1)S(1)}, u32[]{:S(2)}, u32[]{:S(2)}) collective-permute-start(bf16[2,128,256]{2,1,0:T(8,128)(2,1)S(1)} %merge.3), channel_id=1, source_target_pairs={{0,8},{1,9},{2,10},{3,11},{4,12},{5,13},{6,14},{7,15},{8,0},{9,1},... | collective-permute-start | bytes 393224 | tf_op jit(solution)/shard_map/ppermute | solution.py:48
  24.2 1.7 %collective-permute-start.3 = (bf16[128,256]{1,0:T(8,128)(2,1)S(1)}, bf16[128,256]{1,0:T(8,128)(2,1)S(1)}, u32[]{:S(2)}, u32[]{:S(2)}) collective-permute-start(bf16[128,256]{1,0:T(8,128)(2,1)S(1)} %get-tuple-element.20), channel_id=1, source_target_pairs={{0,4},{1,5},{2,6},{3,7},{4,0},{5,1},{6,2},{7,3},{8,12},{9,13},{10,... | collective-permute-start | bytes 196616 | tf_op jit(solution)/shard_map/ppermute | solution.py:48
  25.9 1.5 %collective-permute-start.4 = (bf16[128,256]{1,0:T(8,128)(2,1)S(1)}, bf16[128,256]{1,0:T(8,128)(2,1)S(1)}, u32[]{:S(2)}, u32[]{:S(2)}) collective-permute-start(bf16[128,256]{1,0:T(8,128)(2,1)S(1)} %get-tuple-element.21), channel_id=1, source_target_pairs={{0,1},{1,0},{2,3},{3,2},{4,5},{5,4},{6,7},{7,6},{8,9},{9,8},{10,11... | collective-permute-start | bytes 196616 | tf_op jit(solution)/shard_map/ppermute | solution.py:48
  27.7 0.8 %collective-permute-done.3.refs_5_ = bf16[128,256]{1,0:T(8,128)(2,1)S(1)} collective-permute-done((bf16[128,256]{1,0:T(8,128)(2,1)S(1)}, bf16[128,256]{1,0:T(8,128)(2,1)S(1)}, u32[]{:S(2)}, u32[]{:S(2)}) %collective-permute-start.3) | collective-permute-done | bytes 65568 | tf_op jit(solution)/shard_map/ppermute | solution.py:48
  28.5 2.2 %collective-permute-done.4.refs_6_ = bf16[128,256]{1,0:T(8,128)(2,1)S(1)} collective-permute-done((bf16[128,256]{1,0:T(8,128)(2,1)S(1)}, bf16[128,256]{1,0:T(8,128)(2,1)S(1)}, u32[]{:S(2)}, u32[]{:S(2)}) %collective-permute-start.4) | collective-permute-done | bytes 65568 | tf_op jit(solution)/shard_map/ppermute | solution.py:48
  30.7 1.9 %collective-permute-done.5.refs_7_ = bf16[128,256]{1,0:T(8,128)(2,1)S(1)} collective-permute-done((bf16[128,256]{1,0:T(8,128)(2,1)S(1)}, bf16[128,256]{1,0:T(8,128)(2,1)S(1)}, u32[]{:S(2)}, u32[]{:S(2)}) %collective-permute-start.5) | collective-permute-done | bytes 65568 | tf_op jit(solution)/shard_map/ppermute | solution.py:48
  33.0 0.5 sums.8
  33.5 0.5 %collective-permute-start.11 = (bf16[2,128,256]{2,1,0:T(8,128)(2,1)S(1)}, bf16[2,128,256]{2,1,0:T(8,128)(2,1)S(1)}, u32[]{:S(2)}, u32[]{:S(2)}) collective-permute-start(bf16[2,128,256]{2,1,0:T(8,128)(2,1)S(1)} %get-tuple-element.27), channel_id=1, source_target_pairs={{0,8},{1,9},{2,10},{3,11},{4,12},{5,13},{6,14},{7,15},{8,0},{9,1},... | collective-permute-start | bytes 393224 | tf_op jit(solution)/shard_map/ppermute | solution.py:48
  34.1 2.7 %collective-permute-start.18 = (bf16[128,256]{1,0:T(8,128)(2,1)S(1)}, bf16[128,256]{1,0:T(8,128)(2,1)S(1)}, u32[]{:S(2)}, u32[]{:S(2)}) collective-permute-start(bf16[128,256]{1,0:T(8,128)(2,1)S(1)} %get-tuple-element.35), channel_id=1, source_target_pairs={{0,16},{1,17},{2,18},{3,19},{4,20},{5,21},{6,22},{7,23},{8,24},{9,... | collective-permute-start | bytes 196616 | tf_op jit(solution)/shard_map/ppermute | solution.py:48
  37.4 1.9 %collective-permute-done.18.refs_6_.refs_10_ = bf16[128,256]{1,0:T(8,128)(2,1)S(1)} collective-permute-done((bf16[128,256]{1,0:T(8,128)(2,1)S(1)}, bf16[128,256]{1,0:T(8,128)(2,1)S(1)}, u32[]{:S(2)}, u32[]{:S(2)}) %collective-permute-start.18) | collective-permute-done | bytes 65568 | tf_op jit(solution)/shard_map/ppermute | solution.py:48
  39.3 2.6 %collective-permute-done.11.refs_5_.refs_9_ = bf16[2,128,256]{2,1,0:T(8,128)(2,1)S(1)} collective-permute-done((bf16[2,128,256]{2,1,0:T(8,128)(2,1)S(1)}, bf16[2,128,256]{2,1,0:T(8,128)(2,1)S(1)}, u32[]{:S(2)}, u32[]{:S(2)}) %collective-permute-start.11) | collective-permute-done | bytes 131104 | tf_op jit(solution)/shard_map/ppermute | solution.py:48
  42.1 0.6 %collective-permute-start.20 = (bf16[128,256]{1,0:T(8,128)(2,1)S(1)}, bf16[128,256]{1,0:T(8,128)(2,1)S(1)}, u32[]{:S(2)}, u32[]{:S(2)}) collective-permute-start(bf16[128,256]{1,0:T(8,128)(2,1)S(1)} %adam.4.refs_1_), channel_id=1, source_target_pairs={{0,1},{1,0},{2,3},{3,2},{4,5},{5,4},{6,7},{7,6},{8,9},{9,8},{10,11... | collective-permute-start | bytes 196616 | tf_op jit(solution)/shard_map/ppermute | solution.py:48
  42.7 1.9 %collective-permute-done.17.refs_6_ = bf16[128,256]{1,0:T(8,128)(2,1)S(1)} collective-permute-done((bf16[128,256]{1,0:T(8,128)(2,1)S(1)}, bf16[128,256]{1,0:T(8,128)(2,1)S(1)}, u32[]{:S(2)}, u32[]{:S(2)}) %collective-permute-start.17) | collective-permute-done | bytes 65568 | tf_op jit(solution)/shard_map/ppermute | solution.py:48
  44.8 0.6 %collective-permute-start.19 = (bf16[128,256]{1,0:T(8,128)(2,1)S(1)}, bf16[128,256]{1,0:T(8,128)(2,1)S(1)}, u32[]{:S(2)}, u32[]{:S(2)}) collective-permute-start(bf16[128,256]{1,0:T(8,128)(2,1)S(1)} %adam.3.refs_0_), channel_id=1, source_target_pairs={{0,1},{1,0},{2,3},{3,2},{4,5},{5,4},{6,7},{7,6},{8,9},{9,8},{10,11... | collective-permute-start | bytes 196616 | tf_op jit(solution)/shard_map/ppermute | solution.py:48
  45.5 0.7 %copy.8 = f32[128,512]{1,0:T(8,128)} copy(f32[128,512]{1,0:T(8,128)S(1)} %get-tuple-element.38) | data formatting | bytes 524288
  46.2 0.7 %copy.9 = f32[128,512]{1,0:T(8,128)} copy(f32[128,512]{1,0:T(8,128)S(1)} %get-tuple-element.39) | data formatting | bytes 524288
  46.9 2.2 %collective-permute-done.19.refs_2_ = bf16[128,256]{1,0:T(8,128)(2,1)S(1)} collective-permute-done((bf16[128,256]{1,0:T(8,128)(2,1)S(1)}, bf16[128,256]{1,0:T(8,128)(2,1)S(1)}, u32[]{:S(2)}, u32[]{:S(2)}) %collective-permute-start.19) | collective-permute-done | bytes 65568 | tf_op jit(solution)/shard_map/ppermute | solution.py:48
  49.1 0.7 %join.1 = bf16[256,512]{1,0:T(8,128)(2,1)} custom-call(bf16[128,256]{1,0:T(8,128)(2,1)S(1)} %adam.3.refs_0_, bf16[128,256]{1,0:T(8,128)(2,1)S(1)} %adam.4.refs_1_, bf16[128,256]{1,0:T(8,128)(2,1)S(1)} %collective-permute-done.19.refs_2_, bf16[128,256]{1,0:T(8,128)(2,1)S(1)} %collective-permute-done.20.refs_3_), custom_call_target="tpu_custom_call" | custom-call | tf_op jit(solution)/shard_map/join/pallas_call | solution.py:252
  (34 shorter events, 2.7 us)
Async XLA Ops:
  0.6 17.7 %copy-start = (bf16[128,512]{1,0:T(8,128)(2,1)S(1)}, bf16[128,512]{1,0:T(8,128)(2,1)}, u32[]{:S(2)}) copy-start(bf16[128,512]{1,0:T(8,128)(2,1)} %refs_0_.14) | copy-start | bytes 393220
  0.6 9.6 %collective-permute-start = (bf16[128,512]{1,0:T(8,128)(2,1)}, bf16[128,512]{1,0:T(8,128)(2,1)S(1)}, u32[]{:S(2)}, u32[]{:S(2)}) collective-permute-start(bf16[128,512]{1,0:T(8,128)(2,1)} %refs_0_.14), channel_id=1, source_target_pairs={{0,4},{1,5},{2,6},{3,7},{4,0},{5,1},{6,2},{7,3},{8,12},{9,13},{10,... | collective-permute-start | bytes 393224 | tf_op jit(solution)/shard_map/ppermute | solution.py:48
  3.7 6.6 %collective-permute-start.1 = (bf16[128,512]{1,0:T(8,128)(2,1)}, bf16[128,512]{1,0:T(8,128)(2,1)S(1)}, u32[]{:S(2)}, u32[]{:S(2)}) collective-permute-start(bf16[128,512]{1,0:T(8,128)(2,1)} %refs_0_.14), channel_id=1, source_target_pairs={{0,1},{1,0},{2,3},{3,2},{4,5},{5,4},{6,7},{7,6},{8,9},{9,8},{10,11... | collective-permute-start | bytes 393224 | tf_op jit(solution)/shard_map/ppermute | solution.py:48
  5.2 7.5 %collective-permute-start.2 = (bf16[128,512]{1,0:T(8,128)(2,1)}, bf16[128,512]{1,0:T(8,128)(2,1)S(1)}, u32[]{:S(2)}, u32[]{:S(2)}) collective-permute-start(bf16[128,512]{1,0:T(8,128)(2,1)} %refs_0_.14), channel_id=1, source_target_pairs={{0,5},{1,4},{2,7},{3,6},{4,1},{5,0},{6,3},{7,2},{8,13},{9,12},{10,... | collective-permute-start | bytes 393224 | tf_op jit(solution)/shard_map/ppermute | solution.py:48
  6.8 9.3 %collective-permute-start.7 = (bf16[128,512]{1,0:T(8,128)(2,1)S(1)}, bf16[128,512]{1,0:T(8,128)(2,1)S(1)}, u32[]{:S(2)}, u32[]{:S(2)}) collective-permute-start(bf16[128,512]{1,0:T(8,128)(2,1)S(1)} %get-tuple-element.24), channel_id=1, source_target_pairs={{0,4},{1,5},{2,6},{3,7},{4,0},{5,1},{6,2},{7,3},{8,12},{9,13},{10,... | collective-permute-start | bytes 393224 | tf_op jit(solution)/shard_map/ppermute | solution.py:48
  8.8 9.5 %collective-permute-start.8 = (bf16[128,512]{1,0:T(8,128)(2,1)S(1)}, bf16[128,512]{1,0:T(8,128)(2,1)S(1)}, u32[]{:S(2)}, u32[]{:S(2)}) collective-permute-start(bf16[128,512]{1,0:T(8,128)(2,1)S(1)} %get-tuple-element.25), channel_id=1, source_target_pairs={{0,1},{1,0},{2,3},{3,2},{4,5},{5,4},{6,7},{7,6},{8,9},{9,8},{10,11... | collective-permute-start | bytes 393224 | tf_op jit(solution)/shard_map/ppermute | solution.py:48
  10.3 8.0 %collective-permute-start.9 = (bf16[128,512]{1,0:T(8,128)(2,1)S(1)}, bf16[128,512]{1,0:T(8,128)(2,1)S(1)}, u32[]{:S(2)}, u32[]{:S(2)}) collective-permute-start(bf16[128,512]{1,0:T(8,128)(2,1)S(1)} %get-tuple-element.26), channel_id=1, source_target_pairs={{0,5},{1,4},{2,7},{3,6},{4,1},{5,0},{6,3},{7,2},{8,13},{9,12},{10,... | collective-permute-start | bytes 393224 | tf_op jit(solution)/shard_map/ppermute | solution.py:48
  10.3 8.5 %collective-permute-start.12 = (bf16[128,256]{1,0:T(8,128)(2,1)S(1)}, bf16[128,256]{1,0:T(8,128)(2,1)S(1)}, u32[]{:S(2)}, u32[]{:S(2)}) collective-permute-start(bf16[128,256]{1,0:T(8,128)(2,1)S(1)} %get-tuple-element.30), channel_id=1, source_target_pairs={{0,4},{1,5},{2,6},{3,7},{4,0},{5,1},{6,2},{7,3},{8,12},{9,13},{10,... | collective-permute-start | bytes 196616 | tf_op jit(solution)/shard_map/ppermute | solution.py:48
  12.7 6.7 %collective-permute-start.13 = (bf16[128,256]{1,0:T(8,128)(2,1)S(1)}, bf16[128,256]{1,0:T(8,128)(2,1)S(1)}, u32[]{:S(2)}, u32[]{:S(2)}) collective-permute-start(bf16[128,256]{1,0:T(8,128)(2,1)S(1)} %get-tuple-element.31), channel_id=1, source_target_pairs={{0,1},{1,0},{2,3},{3,2},{4,5},{5,4},{6,7},{7,6},{8,9},{9,8},{10,11... | collective-permute-start | bytes 196616 | tf_op jit(solution)/shard_map/ppermute | solution.py:48
  16.0 5.2 %collective-permute-start.14 = (bf16[128,256]{1,0:T(8,128)(2,1)S(1)}, bf16[128,256]{1,0:T(8,128)(2,1)S(1)}, u32[]{:S(2)}, u32[]{:S(2)}) collective-permute-start(bf16[128,256]{1,0:T(8,128)(2,1)S(1)} %get-tuple-element.32), channel_id=1, source_target_pairs={{0,5},{1,4},{2,7},{3,6},{4,1},{5,0},{6,3},{7,2},{8,13},{9,12},{10,... | collective-permute-start | bytes 196616 | tf_op jit(solution)/shard_map/ppermute | solution.py:48
  18.8 14.7 %collective-permute-start.10 = (bf16[2,256,256]{2,1,0:T(8,128)(2,1)S(1)}, bf16[2,256,256]{2,1,0:T(8,128)(2,1)S(1)}, u32[]{:S(2)}, u32[]{:S(2)}) collective-permute-start(bf16[2,256,256]{2,1,0:T(8,128)(2,1)S(1)} %bitcast.16), channel_id=1, source_target_pairs={{0,2},{1,3},{2,0},{3,1},{4,6},{5,7},{6,4},{7,5},{8,10},{9,11},{10,... | collective-permute-start | bytes 786440 | tf_op jit(solution)/shard_map/ppermute | solution.py:48
  21.5 1.4 %collective-permute-start.15 = (bf16[2,128,256]{2,1,0:T(8,128)(2,1)S(1)}, bf16[2,128,256]{2,1,0:T(8,128)(2,1)S(1)}, u32[]{:S(2)}, u32[]{:S(2)}) collective-permute-start(bf16[2,128,256]{2,1,0:T(8,128)(2,1)S(1)} %bitcast.18), channel_id=1, source_target_pairs={{0,2},{1,3},{2,0},{3,1},{4,6},{5,7},{6,4},{7,5},{8,10},{9,11},{10,... | collective-permute-start | bytes 393224 | tf_op jit(solution)/shard_map/ppermute | solution.py:48
  23.0 11.1 %collective-permute-start.16 = (bf16[2,128,256]{2,1,0:T(8,128)(2,1)S(1)}, bf16[2,128,256]{2,1,0:T(8,128)(2,1)S(1)}, u32[]{:S(2)}, u32[]{:S(2)}) collective-permute-start(bf16[2,128,256]{2,1,0:T(8,128)(2,1)S(1)} %merge.3), channel_id=1, source_target_pairs={{0,8},{1,9},{2,10},{3,11},{4,12},{5,13},{6,14},{7,15},{8,0},{9,1},... | collective-permute-start | bytes 393224 | tf_op jit(solution)/shard_map/ppermute | solution.py:48
  24.2 4.3 %collective-permute-start.3 = (bf16[128,256]{1,0:T(8,128)(2,1)S(1)}, bf16[128,256]{1,0:T(8,128)(2,1)S(1)}, u32[]{:S(2)}, u32[]{:S(2)}) collective-permute-start(bf16[128,256]{1,0:T(8,128)(2,1)S(1)} %get-tuple-element.20), channel_id=1, source_target_pairs={{0,4},{1,5},{2,6},{3,7},{4,0},{5,1},{6,2},{7,3},{8,12},{9,13},{10,... | collective-permute-start | bytes 196616 | tf_op jit(solution)/shard_map/ppermute | solution.py:48
  25.9 4.7 %collective-permute-start.4 = (bf16[128,256]{1,0:T(8,128)(2,1)S(1)}, bf16[128,256]{1,0:T(8,128)(2,1)S(1)}, u32[]{:S(2)}, u32[]{:S(2)}) collective-permute-start(bf16[128,256]{1,0:T(8,128)(2,1)S(1)} %get-tuple-element.21), channel_id=1, source_target_pairs={{0,1},{1,0},{2,3},{3,2},{4,5},{5,4},{6,7},{7,6},{8,9},{9,8},{10,11... | collective-permute-start | bytes 196616 | tf_op jit(solution)/shard_map/ppermute | solution.py:48
  27.4 5.2 %collective-permute-start.5 = (bf16[128,256]{1,0:T(8,128)(2,1)S(1)}, bf16[128,256]{1,0:T(8,128)(2,1)S(1)}, u32[]{:S(2)}, u32[]{:S(2)}) collective-permute-start(bf16[128,256]{1,0:T(8,128)(2,1)S(1)} %get-tuple-element.22), channel_id=1, source_target_pairs={{0,5},{1,4},{2,7},{3,6},{4,1},{5,0},{6,3},{7,2},{8,13},{9,12},{10,... | collective-permute-start | bytes 196616 | tf_op jit(solution)/shard_map/ppermute | solution.py:48
  32.9 4.5 %collective-permute-start.6 = (bf16[2,128,256]{2,1,0:T(8,128)(2,1)S(1)}, bf16[2,128,256]{2,1,0:T(8,128)(2,1)S(1)}, u32[]{:S(2)}, u32[]{:S(2)}) collective-permute-start(bf16[2,128,256]{2,1,0:T(8,128)(2,1)S(1)} %bitcast.17), channel_id=1, source_target_pairs={{0,2},{1,3},{2,0},{3,1},{4,6},{5,7},{6,4},{7,5},{8,10},{9,11},{10,... | collective-permute-start | bytes 393224 | tf_op jit(solution)/shard_map/ppermute | solution.py:48
  33.5 8.5 %collective-permute-start.11 = (bf16[2,128,256]{2,1,0:T(8,128)(2,1)S(1)}, bf16[2,128,256]{2,1,0:T(8,128)(2,1)S(1)}, u32[]{:S(2)}, u32[]{:S(2)}) collective-permute-start(bf16[2,128,256]{2,1,0:T(8,128)(2,1)S(1)} %get-tuple-element.27), channel_id=1, source_target_pairs={{0,8},{1,9},{2,10},{3,11},{4,12},{5,13},{6,14},{7,15},{8,0},{9,1},... | collective-permute-start | bytes 393224 | tf_op jit(solution)/shard_map/ppermute | solution.py:48
  34.1 5.3 %collective-permute-start.18 = (bf16[128,256]{1,0:T(8,128)(2,1)S(1)}, bf16[128,256]{1,0:T(8,128)(2,1)S(1)}, u32[]{:S(2)}, u32[]{:S(2)}) collective-permute-start(bf16[128,256]{1,0:T(8,128)(2,1)S(1)} %get-tuple-element.35), channel_id=1, source_target_pairs={{0,16},{1,17},{2,18},{3,19},{4,20},{5,21},{6,22},{7,23},{8,24},{9,... | collective-permute-start | bytes 196616 | tf_op jit(solution)/shard_map/ppermute | solution.py:48
  36.7 5.3 %copy-start.1 = (f32[128,512]{1,0:T(8,128)S(1)}, f32[128,512]{1,0:T(8,128)}, u32[]{:S(2)}) copy-start(f32[128,512]{1,0:T(8,128)} %refs_0_.17) | copy-start | bytes 786436
  36.7 5.3 %copy-start.2 = (f32[128,512]{1,0:T(8,128)S(1)}, f32[128,512]{1,0:T(8,128)}, u32[]{:S(2)}) copy-start(f32[128,512]{1,0:T(8,128)} %refs_1_.5) | copy-start | bytes 786436
  36.7 5.3 %copy-start.3 = (f32[128,512]{1,0:T(8,128)S(1)}, f32[128,512]{1,0:T(8,128)}, u32[]{:S(2)}) copy-start(f32[128,512]{1,0:T(8,128)} %refs_2_.5) | copy-start | bytes 786436
  36.7 7.9 %collective-permute-start.17 = (bf16[128,256]{1,0:T(8,128)(2,1)S(1)}, bf16[128,256]{1,0:T(8,128)(2,1)S(1)}, u32[]{:S(2)}, u32[]{:S(2)}) collective-permute-start(bf16[128,256]{1,0:T(8,128)(2,1)S(1)} %get-tuple-element.36), channel_id=1, source_target_pairs={{0,16},{1,17},{2,18},{3,19},{4,20},{5,21},{6,22},{7,23},{8,24},{9,... | collective-permute-start | bytes 196616 | tf_op jit(solution)/shard_map/ppermute | solution.py:48
  42.1 4.8 %collective-permute-start.20 = (bf16[128,256]{1,0:T(8,128)(2,1)S(1)}, bf16[128,256]{1,0:T(8,128)(2,1)S(1)}, u32[]{:S(2)}, u32[]{:S(2)}) collective-permute-start(bf16[128,256]{1,0:T(8,128)(2,1)S(1)} %adam.4.refs_1_), channel_id=1, source_target_pairs={{0,1},{1,0},{2,3},{3,2},{4,5},{5,4},{6,7},{7,6},{8,9},{9,8},{10,11... | collective-permute-start | bytes 196616 | tf_op jit(solution)/shard_map/ppermute | solution.py:48
  44.8 4.3 %collective-permute-start.19 = (bf16[128,256]{1,0:T(8,128)(2,1)S(1)}, bf16[128,256]{1,0:T(8,128)(2,1)S(1)}, u32[]{:S(2)}, u32[]{:S(2)}) collective-permute-start(bf16[128,256]{1,0:T(8,128)(2,1)S(1)} %adam.3.refs_0_), channel_id=1, source_target_pairs={{0,1},{1,0},{2,3},{3,2},{4,5},{5,4},{6,7},{7,6},{8,9},{9,8},{10,11... | collective-permute-start | bytes 196616 | tf_op jit(solution)/shard_map/ppermute | solution.py:48
where the time goes:
time: 50 us; the launch traced here: 49.8 us
  starting transfers between devices  23.8 us (48%)
  waiting for transfers between devices  18.9 us (38%)
  Pallas kernels  4.87 us (10%)
  local copies, waits for them, and re-layouts  1.42 us (3%)
  between operations  0.79 us (2%)
    ppermute x21, starting transfers between devices, permute(): return lax.ppermute(value, ('node', 'local'), pairs)  23.8 us
    ppermute x21, waiting for transfers between devices, permute(): return lax.ppermute(value, ('node', 'local'), pairs)  18.9 us
    pallas_call x6, Pallas kernels, group_sums(): pl.pallas_call(functools.partial(sums_kernel, len(rights), cores, size),...  2.17 us
    pallas_call x1, Pallas kernels, take(): pl.pallas_call(functools.partial(take_kernel, grid, wanted, rows), out_sh...  1.5 us
    unnamed x10, local copies, waits for them, and re-layouts  1.42 us
  transfers between devices with their start and end apart: 21, of which 12 were waited for; matrix products, arithmetic and copies ran while one was open for 3% of the time, Pallas kernels for 8%

commit v1 on v0

v1 whole, which is shorter than its diff:
```python
import functools

import jax
import jax.numpy as jnp
from jax import lax
from jax.experimental import pallas as pl
from jax.experimental.pallas import tpu as pltpu
from jax.sharding import PartitionSpec as P


def partner(index, step, count):
    if count & (count - 1) == 0:
        return index ^ step
    return (index + step) % count


class Layout:
    def __init__(self, node_count, local_count):
        self.core = 2 if node_count % 2 == 0 else 1
        rest = node_count // self.core
        self.middle = 2 if rest % 2 == 0 else 1
        self.outer = rest // self.middle
        if self.outer & (self.outer - 1):
            self.middle, self.outer = rest, 1
        self.local = local_count
        self.group = self.middle * self.local

    def split(self, device):
        node, local = device // self.local, device % self.local
        core, rest = node % self.core, node // self.core
        return rest // self.middle, rest % self.middle, core, local

    def join(self, outer, middle, core, local):
        return ((outer * self.middle + middle) * self.core + core) * self.local + local

    def move(self, device, outer=0, group=0, core=0):
        o, m, c, l = self.split(device)
        return self.join(
            partner(o, outer, self.outer),
            partner(m, group // self.local, self.middle),
            partner(c, core, self.core),
            partner(l, group % self.local, self.local),
        )

    def permute(self, value, **steps):
        count = self.outer * self.middle * self.core * self.local
        pairs = [(d, self.move(d, **steps)) for d in range(count)]
        return lax.ppermute(value, ("node", "local"), pairs)

    def peers(self):
        both = [(g // self.local, g % self.local) for g in range(1, self.group)]
        both.sort(key=lambda ml: (ml[0] > 0 and ml[1] > 0, ml[1] > 0))
        return tuple(m * self.local + l for m, l in both)

    def me(self):
        return lax.axis_index("node") * self.local + lax.axis_index("local")


def in_vmem(value):
    return pltpu.with_memory_space_constraint(value, pltpu.VMEM)


CUT = 4
SMALL = pltpu.CompilerParams(vmem_limit_bytes=16 * 2**20)


def take_kernel(grid, wanted, rows, source, *outs):
    me = grid.me()
    for (group, steps), out in zip(wanted, outs):
        for j, (o, c) in enumerate((o, c) for c in range(grid.core) for o in steps):
            block = grid.move(me, outer=o, group=group, core=c)
            columns = pl.ds(pl.multiple_of(block * rows, rows), rows)
            out[:, pl.ds(j * rows, rows)] = source[:, columns]


def take(grid, wanted, rows, activations):
    tokens = activations.shape[0]
    if rows % 128:
        me = grid.me()
        out = []
        for group, steps in wanted:
            blocks = [
                grid.move(me, outer=o, group=group, core=c) for c in range(grid.core) for o in steps
            ]
            parts = [lax.dynamic_slice_in_dim(activations, b * rows, rows, 1) for b in blocks]
            out.append(jnp.concatenate(parts, 1))
        return out
    return pl.pallas_call(
        functools.partial(take_kernel, grid, wanted, rows),
        out_shape=[
            pltpu.VMEM((tokens, len(steps) * grid.core * rows), activations.dtype)
            for _, steps in wanted
        ],
        in_specs=[pl.BlockSpec(memory_space=pltpu.VMEM)],
        out_specs=[pl.BlockSpec(memory_space=pltpu.VMEM)] * len(wanted),
        compiler_params=SMALL,
        name="take",
    )(in_vmem(activations))


def product(left, right):
    return lax.dot_general(
        left, right, (((0,), (0,)), ((), ())), preferred_element_type=jnp.float32
    )


def sums_kernel(members, firsts, *refs):
    rights, lefts, out = refs[:members], refs[members:-1], refs[-1]
    size = out.shape[1]
    for j, first in enumerate(firsts):
        total = None
        for left, right in zip(lefts, rights):
            part = product(left[:, pl.ds(first, size)], right[...])
            total = part if total is None else total + part
        out[j] = total.astype(out.dtype)


def group_sums(firsts, size, dtype, rights, lefts):
    cols = rights[0].shape[1]
    if size % 128:
        left, right = jnp.concatenate(lefts, 0), jnp.concatenate(rights, 0)
        return jnp.stack([product(left[:, f : f + size], right).astype(dtype) for f in firsts])
    vmem = pl.BlockSpec(memory_space=pltpu.VMEM)
    operands = (*rights, *lefts)
    return pl.pallas_call(
        functools.partial(sums_kernel, len(rights), firsts),
        out_shape=pltpu.VMEM((len(firsts), size, cols), dtype),
        in_specs=[vmem] * len(operands),
        out_specs=vmem,
        compiler_params=SMALL,
        name="sums",
    )(*(in_vmem(v) for v in operands))


def adam(grad, master, first_moment, second_moment):
    new_first = 0.9 * first_moment + 0.1 * grad
    new_second = 0.95 * second_moment + 0.05 * grad * grad
    update = new_first / (1.0 - 0.9**10) / (jnp.sqrt(new_second / (1.0 - 0.95**10)) + 1e-08)
    return (master - 0.01 * update).astype(jnp.bfloat16), new_first, new_second


def update_kernel(count, cuts, weights, shared, *refs):
    master, first_moment, second_moment = refs[:3]
    common, refs = refs[3 : 3 + shared], refs[3 + shared :]
    outs = refs[-1:] if weights else refs[-2:]
    own = (len(refs) - len(outs)) // len(cuts)
    for i, (start, width) in enumerate(cuts):
        at = pl.ds(start, width)
        total = common[0][:, at]
        for part in common[1:]:
            total += part[:, at].astype(jnp.float32)
        for part in refs[i * own : (i + 1) * own]:
            total += part[...].astype(jnp.float32)
        step = adam(total / count, master[:, at], first_moment[:, at], second_moment[:, at])
        if weights:
            outs[0][...] = step[0]
        else:
            outs[0][:, at] = step[1]
            outs[1][:, at] = step[2]


def update(count, cuts, weights, state, common, parts):
    rows, cols = state[0].shape
    if rows % 128:
        out = []
        for (start, width), part in zip(cuts, parts):
            at = slice(start, start + width)
            total = sum([v[:, at].astype(jnp.float32) for v in common])
            total = sum([v.astype(jnp.float32) for v in part], total)
            out.append(adam(total / count, *(v[:, at] for v in state)))
        return [jnp.concatenate([o[i] for o in out], 1) for i in ((0,) if weights else (1, 2))]
    vmem = pl.BlockSpec(memory_space=pltpu.VMEM)
    operands = [*state, *common, *(v for part in parts for v in part)]
    if weights:
        out_shape = [pltpu.VMEM((rows, cuts[0][1]), jnp.bfloat16)]
    else:
        out_shape = [pltpu.VMEM((rows, cols), jnp.float32)] * 2
    return pl.pallas_call(
        functools.partial(update_kernel, count, cuts, weights, len(common)),
        out_shape=out_shape,
        in_specs=[vmem] * len(operands),
        out_specs=[vmem] * len(out_shape),
        compiler_params=SMALL,
        name="adam",
    )(*(in_vmem(v) for v in operands))


def join_kernel(*refs):
    *parts, out, sems = refs
    rows = parts[0].shape[0]
    mine = lax.axis_index("local")
    copies = []
    for i, row in enumerate((mine, 1 - mine)):
        start = 0
        for part in parts[i * len(parts) // 2 : (i + 1) * len(parts) // 2]:
            columns = pl.ds(start, part.shape[1])
            copies.append(
                pltpu.make_async_copy(
                    part, out.at[pl.ds(row * rows, rows), columns], sems.at[len(copies)]
                )
            )
            start += part.shape[1]
    for copy in copies:
        copy.start()
    for copy in copies:
        copy.wait()


def joined(grid, own):
    rows = own[0].shape[0]
    if grid.local != 2 or rows % 128:
        return lax.all_gather(jnp.concatenate(own, 1), "local", axis=0, tiled=True)
    other = []
    for part in own:
        other.append(grid.permute(part, group=1))
    vmem = pl.BlockSpec(memory_space=pltpu.VMEM)
    operands = (*own, *other)
    return pl.pallas_call(
        join_kernel,
        out_shape=jax.ShapeDtypeStruct((2 * rows, sum(p.shape[1] for p in own)), own[0].dtype),
        in_specs=[vmem] * len(operands),
        out_specs=pl.BlockSpec(memory_space=pl.ANY),
        scratch_shapes=[pltpu.SemaphoreType.DMA((len(operands),))],
        compiler_params=SMALL,
        name="join",
    )(*(in_vmem(v) for v in operands))


def step(activations, out_grads, *state):
    grid = Layout(lax.axis_size("node"), lax.axis_size("local"))
    rows = state[0].shape[0]
    count = grid.outer * grid.middle * grid.core * grid.local
    groups = grid.peers()
    odd, even = tuple(range(3, grid.outer, 2)), tuple(range(2, grid.outer, 2))
    near = tuple(range(1, min(2, grid.outer)))

    def send(messages):
        out = []
        for g, message in zip(groups, messages):
            out.append(grid.permute(message, group=g))
        return out

    rights = [out_grads] + send([out_grads] * len(groups))
    plan = {"a": odd, "b": even + near, "c": (0,)}
    plan = {name: steps for name, steps in plan.items() if steps}
    peers = (*groups, 0)
    taken = take(grid, [(g, steps) for steps in plan.values() for g in peers], rows, activations)
    lefts = {}
    for j, name in enumerate(plan):
        *messages, own = taken[j * len(peers) : (j + 1) * len(peers)]
        lefts[name] = [own] + send(messages)

    half, full = jnp.bfloat16, jnp.float32

    def sums(message, skip=0, steps=None):
        stride = len(plan[message]) * rows
        size = stride if steps is None else len(steps) * rows
        operands = rights, lefts[message]
        got = []
        if grid.core > 1:
            firsts = tuple(c * stride + skip * rows for c in range(1, grid.core))
            sent = group_sums(firsts, size, half, *operands)
            got = [grid.permute(sent[c], core=c + 1) for c in range(grid.core - 1)]
        kept = group_sums((skip * rows,), size, full, *operands)[0]
        return [kept, *got]

    def hop(parts, outer):
        part = sum([p.astype(full) for p in parts[1:]], parts[0])
        return grid.permute(part.astype(half), outer=outer)

    cols = out_grads.shape[1]
    most = cols - max(cols // CUT, 1)
    cuts = ((0, most), (most, cols - most))
    common, parts = [], [[], []]
    if odd:
        passed = hop(sums("a"), 1)
    if near:
        common.append(hop(sums("b", len(even), near), 1))
    if odd:
        total = [*sums("b", 0, even), passed]
        for j, (start, width) in enumerate(cuts):
            for i, o in enumerate(even):
                part = [p[i * rows : (i + 1) * rows, start : start + width] for p in total]
                parts[j].append(hop(part, o))
    common = sums("c") + common

    weights = []
    for j in range(2):
        weights += update(count, cuts[j : j + 1], True, state, common, parts[j : j + 1])
    new_first, new_second = update(count, cuts, False, state, common, parts)
    new_weight = joined(grid, weights)
    return (new_weight, new_first, new_second)


def solution(mesh):
    spec = P(("node", "local"), None)
    return jax.shard_map(
        step,
        mesh=mesh,
        in_specs=(spec,) * 5,
        out_specs=(P("node", None), spec, spec),
        check_vma=False,
    )
```

time: 50 us -> 53.7 us (1.074)
  waiting for transfers between devices: 18.9 us -> 21 us
  local copies, waits for them, and re-layouts: 1.42 us -> 2.68 us
  starting transfers between devices: 23.8 us -> 25 us
  Pallas kernels: 4.87 us -> 3.92 us
    ppermute x21 -> x22, waiting for transfers between devices: 18.9 us -> 21 us  [permute(): return lax.ppermute(value, ('node', 'local'), pairs)]
    unnamed x10 -> x12, local copies, waits for them, and re-layouts: 1.42 us -> 2.68 us
    pallas_call x1, Pallas kernels: 1.5 us -> 0.27 us  [take(): pl.pallas_call(functools.partial(take_kernel, grid, wanted, rows), out_sh...]
    ppermute x21 -> x22, starting transfers between devices: 23.8 us -> 25 us  [permute(): return lax.ppermute(value, ('node', 'local'), pairs)]
  transfers between devices with their start and end apart: 21 -> 22, of which waited for: 12 -> 10; matrix products, arithmetic and copies ran while one was open for 3% -> 3% of each run, Pallas kernels for 8% -> 5%
where the time goes in v1:
time: 53.7 us; the launch traced here: 53.5 us
  starting transfers between devices  25 us (47%)
  waiting for transfers between devices  21 us (39%)
  Pallas kernels  3.92 us (7%)
  local copies, waits for them, and re-layouts  2.68 us (5%)
  between operations  0.84 us (2%)
    ppermute x22, starting transfers between devices, permute(): return lax.ppermute(value, ('node', 'local'), pairs)  25 us
    ppermute x22, waiting for transfers between devices, permute(): return lax.ppermute(value, ('node', 'local'), pairs)  21 us
    unnamed x12, local copies, waits for them, and re-layouts  2.68 us
    pallas_call x8, Pallas kernels, group_sums(): pl.pallas_call(functools.partial(sums_kernel, len(rights), firsts), out_s...  2.51 us
  transfers between devices with their start and end apart: 22, of which 10 were waited for; matrix products, arithmetic and copies ran while one was open for 3% of the time, Pallas kernels for 5%

profile of v1, /device:TPU:0, one launch (start us, length us, event | category | flops | bytes accessed | tf_op | source)
XLA Modules:
  0.0 53.5 jit_solution(9342323260747656123)
XLA Ops:
  0.6 1.3 %copy-done.4 = bf16[128,4096]{1,0:T(8,128)(2,1)S(1)} copy-done((bf16[128,4096]{1,0:T(8,128)(2,1)S(1)}, bf16[128,4096]{1,0:T(8,128)(2,1)}, u32[]{:S(2)}) %copy-start.4) | copy-done | bytes 1048600
  2.2 3.1 %collective-permute-start.13 = (bf16[128,256]{1,0:T(8,128)(2,1)S(1)}, bf16[128,256]{1,0:T(8,128)(2,1)S(1)}, u32[]{:S(2)}, u32[]{:S(2)}) collective-permute-start(bf16[128,256]{1,0:T(8,128)(2,1)S(1)} %get-tuple-element.26), channel_id=1, source_target_pairs={{0,4},{1,5},{2,6},{3,7},{4,0},{5,1},{6,2},{7,3},{8,12},{9,13},{10,... | collective-permute-start | bytes 196616 | tf_op jit(solution)/shard_map/ppermute | solution.py:48
  5.3 1.9 %collective-permute-start.14 = (bf16[128,256]{1,0:T(8,128)(2,1)S(1)}, bf16[128,256]{1,0:T(8,128)(2,1)S(1)}, u32[]{:S(2)}, u32[]{:S(2)}) collective-permute-start(bf16[128,256]{1,0:T(8,128)(2,1)S(1)} %get-tuple-element.27), channel_id=1, source_target_pairs={{0,1},{1,0},{2,3},{3,2},{4,5},{5,4},{6,7},{7,6},{8,9},{9,8},{10,11... | collective-permute-start | bytes 196616 | tf_op jit(solution)/shard_map/ppermute | solution.py:48
  7.2 1.5 %collective-permute-start.15 = (bf16[128,256]{1,0:T(8,128)(2,1)S(1)}, bf16[128,256]{1,0:T(8,128)(2,1)S(1)}, u32[]{:S(2)}, u32[]{:S(2)}) collective-permute-start(bf16[128,256]{1,0:T(8,128)(2,1)S(1)} %get-tuple-element.28), channel_id=1, source_target_pairs={{0,5},{1,4},{2,7},{3,6},{4,1},{5,0},{6,3},{7,2},{8,13},{9,12},{10,... | collective-permute-start | bytes 196616 | tf_op jit(solution)/shard_map/ppermute | solution.py:48
  8.7 1.5 %collective-permute-start.1 = (bf16[128,512]{1,0:T(8,128)(2,1)S(1)}, bf16[128,512]{1,0:T(8,128)(2,1)S(1)}, u32[]{:S(2)}, u32[]{:S(2)}) collective-permute-start(bf16[128,512]{1,0:T(8,128)(2,1)S(1)} %copy-done), channel_id=1, source_target_pairs={{0,1},{1,0},{2,3},{3,2},{4,5},{5,4},{6,7},{7,6},{8,9},{9,8},{10,11... | collective-permute-start | bytes 393224 | tf_op jit(solution)/shard_map/ppermute | solution.py:48
  10.2 0.9 %collective-permute-start.2 = (bf16[128,512]{1,0:T(8,128)(2,1)S(1)}, bf16[128,512]{1,0:T(8,128)(2,1)S(1)}, u32[]{:S(2)}, u32[]{:S(2)}) collective-permute-start(bf16[128,512]{1,0:T(8,128)(2,1)S(1)} %copy-done), channel_id=1, source_target_pairs={{0,5},{1,4},{2,7},{3,6},{4,1},{5,0},{6,3},{7,2},{8,13},{9,12},{10,... | collective-permute-start | bytes 393224 | tf_op jit(solution)/shard_map/ppermute | solution.py:48
  11.1 1.1 %collective-permute-start.7 = (bf16[128,512]{1,0:T(8,128)(2,1)S(1)}, bf16[128,512]{1,0:T(8,128)(2,1)S(1)}, u32[]{:S(2)}, u32[]{:S(2)}) collective-permute-start(bf16[128,512]{1,0:T(8,128)(2,1)S(1)} %get-tuple-element.22), channel_id=1, source_target_pairs={{0,4},{1,5},{2,6},{3,7},{4,0},{5,1},{6,2},{7,3},{8,12},{9,13},{10,... | collective-permute-start | bytes 393224 | tf_op jit(solution)/shard_map/ppermute | solution.py:48
  12.2 0.9 %collective-permute-done.15.refs_7_ = bf16[128,256]{1,0:T(8,128)(2,1)S(1)} collective-permute-done((bf16[128,256]{1,0:T(8,128)(2,1)S(1)}, bf16[128,256]{1,0:T(8,128)(2,1)S(1)}, u32[]{:S(2)}, u32[]{:S(2)}) %collective-permute-start.15) | collective-permute-done | bytes 65568 | tf_op jit(solution)/shard_map/ppermute | solution.py:48
  13.1 1.6 %collective-permute-start.8 = (bf16[128,512]{1,0:T(8,128)(2,1)S(1)}, bf16[128,512]{1,0:T(8,128)(2,1)S(1)}, u32[]{:S(2)}, u32[]{:S(2)}) collective-permute-start(bf16[128,512]{1,0:T(8,128)(2,1)S(1)} %get-tuple-element.23), channel_id=1, source_target_pairs={{0,1},{1,0},{2,3},{3,2},{4,5},{5,4},{6,7},{7,6},{8,9},{9,8},{10,11... | collective-permute-start | bytes 393224 | tf_op jit(solution)/shard_map/ppermute | solution.py:48
  14.7 1.5 %collective-permute-start.9 = (bf16[128,512]{1,0:T(8,128)(2,1)S(1)}, bf16[128,512]{1,0:T(8,128)(2,1)S(1)}, u32[]{:S(2)}, u32[]{:S(2)}) collective-permute-start(bf16[128,512]{1,0:T(8,128)(2,1)S(1)} %get-tuple-element.24), channel_id=1, source_target_pairs={{0,5},{1,4},{2,7},{3,6},{4,1},{5,0},{6,3},{7,2},{8,13},{9,12},{10,... | collective-permute-start | bytes 393224 | tf_op jit(solution)/shard_map/ppermute | solution.py:48
  16.2 2.5 %collective-permute-done.2.refs_3_ = bf16[128,512]{1,0:T(8,128)(2,1)S(1)} collective-permute-done((bf16[128,512]{1,0:T(8,128)(2,1)S(1)}, bf16[128,512]{1,0:T(8,128)(2,1)S(1)}, u32[]{:S(2)}, u32[]{:S(2)}) %collective-permute-start.2) | collective-permute-done | bytes 131104 | tf_op jit(solution)/shard_map/ppermute | solution.py:48
  19.1 1.6 %collective-permute-start.3 = (bf16[128,256]{1,0:T(8,128)(2,1)S(1)}, bf16[128,256]{1,0:T(8,128)(2,1)S(1)}, u32[]{:S(2)}, u32[]{:S(2)}) collective-permute-start(bf16[128,256]{1,0:T(8,128)(2,1)S(1)} %get-tuple-element.18), channel_id=1, source_target_pairs={{0,4},{1,5},{2,6},{3,7},{4,0},{5,1},{6,2},{7,3},{8,12},{9,13},{10,... | collective-permute-start | bytes 196616 | tf_op jit(solution)/shard_map/ppermute | solution.py:48
  20.8 0.6 %collective-permute-start.4 = (bf16[128,256]{1,0:T(8,128)(2,1)S(1)}, bf16[128,256]{1,0:T(8,128)(2,1)S(1)}, u32[]{:S(2)}, u32[]{:S(2)}) collective-permute-start(bf16[128,256]{1,0:T(8,128)(2,1)S(1)} %get-tuple-element.19), channel_id=1, source_target_pairs={{0,1},{1,0},{2,3},{3,2},{4,5},{5,4},{6,7},{7,6},{8,9},{9,8},{10,11... | collective-permute-start | bytes 196616 | tf_op jit(solution)/shard_map/ppermute | solution.py:48
  21.3 1.4 %collective-permute-start.5 = (bf16[128,256]{1,0:T(8,128)(2,1)S(1)}, bf16[128,256]{1,0:T(8,128)(2,1)S(1)}, u32[]{:S(2)}, u32[]{:S(2)}) collective-permute-start(bf16[128,256]{1,0:T(8,128)(2,1)S(1)} %get-tuple-element.20), channel_id=1, source_target_pairs={{0,5},{1,4},{2,7},{3,6},{4,1},{5,0},{6,3},{7,2},{8,13},{9,12},{10,... | collective-permute-start | bytes 196616 | tf_op jit(solution)/shard_map/ppermute | solution.py:48
  22.7 0.4 collective-permute-done.9.refs_7_
  23.5 0.3 sums.11
  23.8 0.7 %collective-permute-done.3.refs_5_ = bf16[128,256]{1,0:T(8,128)(2,1)S(1)} collective-permute-done((bf16[128,256]{1,0:T(8,128)(2,1)S(1)}, bf16[128,256]{1,0:T(8,128)(2,1)S(1)}, u32[]{:S(2)}, u32[]{:S(2)}) %collective-permute-start.3) | collective-permute-done | bytes 65568 | tf_op jit(solution)/shard_map/ppermute | solution.py:48
  24.6 0.9 %collective-permute-done.4.refs_6_ = bf16[128,256]{1,0:T(8,128)(2,1)S(1)} collective-permute-done((bf16[128,256]{1,0:T(8,128)(2,1)S(1)}, bf16[128,256]{1,0:T(8,128)(2,1)S(1)}, u32[]{:S(2)}, u32[]{:S(2)}) %collective-permute-start.4) | collective-permute-done | bytes 65568 | tf_op jit(solution)/shard_map/ppermute | solution.py:48
  25.5 1.0 %collective-permute-done.5.refs_7_ = bf16[128,256]{1,0:T(8,128)(2,1)S(1)} collective-permute-done((bf16[128,256]{1,0:T(8,128)(2,1)S(1)}, bf16[128,256]{1,0:T(8,128)(2,1)S(1)}, u32[]{:S(2)}, u32[]{:S(2)}) %collective-permute-start.5) | collective-permute-done | bytes 65568 | tf_op jit(solution)/shard_map/ppermute | solution.py:48
  27.9 1.6 %collective-permute-start.17 = (bf16[128,512]{1,0:T(8,128)(2,1)S(1)}, bf16[128,512]{1,0:T(8,128)(2,1)S(1)}, u32[]{:S(2)}, u32[]{:S(2)}) collective-permute-start(bf16[128,512]{1,0:T(8,128)(2,1)S(1)} %fusion), channel_id=1, source_target_pairs={{0,8},{1,9},{2,10},{3,11},{4,12},{5,13},{6,14},{7,15},{8,0},{9,1},... | collective-permute-start | bytes 393224 | tf_op jit(solution)/shard_map/ppermute | solution.py:48
  29.6 0.5 collective-permute-start.11
  30.1 4.2 %collective-permute-done.17 = bf16[128,512]{1,0:T(8,128)(2,1)S(1)} collective-permute-done((bf16[128,512]{1,0:T(8,128)(2,1)S(1)}, bf16[128,512]{1,0:T(8,128)(2,1)S(1)}, u32[]{:S(2)}, u32[]{:S(2)}) %collective-permute-start.17) | collective-permute-done | bytes 131104 | tf_op jit(solution)/shard_map/ppermute | solution.py:48
  34.4 2.7 %collective-permute-start.18 = (bf16[128,384]{1,0:T(8,128)(2,1)S(1)}, bf16[128,384]{1,0:T(8,128)(2,1)S(1)}, u32[]{:S(2)}, u32[]{:S(2)}) collective-permute-start(bf16[128,384]{1,0:T(8,128)(2,1)S(1)} %fusion.3), channel_id=1, source_target_pairs={{0,16},{1,17},{2,18},{3,19},{4,20},{5,21},{6,22},{7,23},{8,24},{9,... | collective-permute-start | bytes 294920 | tf_op jit(solution)/shard_map/ppermute | solution.py:48
  37.4 4.3 %collective-permute-done.18.refs_6_ = bf16[128,384]{1,0:T(8,128)(2,1)S(1)} collective-permute-done((bf16[128,384]{1,0:T(8,128)(2,1)S(1)}, bf16[128,384]{1,0:T(8,128)(2,1)S(1)}, u32[]{:S(2)}, u32[]{:S(2)}) %collective-permute-start.18) | collective-permute-done | bytes 98336 | tf_op jit(solution)/shard_map/ppermute | solution.py:48
  42.0 1.5 %collective-permute-start.20 = (bf16[128,384]{1,0:T(8,128)(2,1)S(1)}, bf16[128,384]{1,0:T(8,128)(2,1)S(1)}, u32[]{:S(2)}, u32[]{:S(2)}) collective-permute-start(bf16[128,384]{1,0:T(8,128)(2,1)S(1)} %adam.3.refs_0_), channel_id=1, source_target_pairs={{0,1},{1,0},{2,3},{3,2},{4,5},{5,4},{6,7},{7,6},{8,9},{9,8},{10,11... | collective-permute-start | bytes 294920 | tf_op jit(solution)/shard_map/ppermute | solution.py:48
  43.5 1.0 %collective-permute-start.19 = (bf16[128,128]{1,0:T(8,128)(2,1)S(1)}, bf16[128,128]{1,0:T(8,128)(2,1)S(1)}, u32[]{:S(2)}, u32[]{:S(2)}) collective-permute-start(bf16[128,128]{1,0:T(8,128)(2,1)S(1)} %fusion.5), channel_id=1, source_target_pairs={{0,16},{1,17},{2,18},{3,19},{4,20},{5,21},{6,22},{7,23},{8,24},{9,... | collective-permute-start | bytes 98312 | tf_op jit(solution)/shard_map/ppermute | solution.py:48
  44.5 4.3 %collective-permute-done.19.refs_6_.refs_7_ = bf16[128,128]{1,0:T(8,128)(2,1)S(1)} collective-permute-done((bf16[128,128]{1,0:T(8,128)(2,1)S(1)}, bf16[128,128]{1,0:T(8,128)(2,1)S(1)}, u32[]{:S(2)}, u32[]{:S(2)}) %collective-permute-start.19) | collective-permute-done | bytes 32800 | tf_op jit(solution)/shard_map/ppermute | solution.py:48
  48.8 0.7 %collective-permute-start.21 = (bf16[128,128]{1,0:T(8,128)(2,1)S(1)}, bf16[128,128]{1,0:T(8,128)(2,1)S(1)}, u32[]{:S(2)}, u32[]{:S(2)}) collective-permute-start(bf16[128,128]{1,0:T(8,128)(2,1)S(1)} %adam.4.refs_1_), channel_id=1, source_target_pairs={{0,1},{1,0},{2,3},{3,2},{4,5},{5,4},{6,7},{7,6},{8,9},{9,8},{10,11... | collective-permute-start | bytes 98312 | tf_op jit(solution)/shard_map/ppermute | solution.py:48
  49.6 0.7 %copy.8 = f32[128,512]{1,0:T(8,128)} copy(f32[128,512]{1,0:T(8,128)S(1)} %get-tuple-element.32) | data formatting | bytes 524288
  50.3 0.7 %copy.9 = f32[128,512]{1,0:T(8,128)} copy(f32[128,512]{1,0:T(8,128)S(1)} %get-tuple-element.33) | data formatting | bytes 524288
  51.0 1.8 %collective-permute-done.21.refs_3_ = bf16[128,128]{1,0:T(8,128)(2,1)S(1)} collective-permute-done((bf16[128,128]{1,0:T(8,128)(2,1)S(1)}, bf16[128,128]{1,0:T(8,128)(2,1)S(1)}, u32[]{:S(2)}, u32[]{:S(2)}) %collective-permute-start.21) | collective-permute-done | bytes 32800 | tf_op jit(solution)/shard_map/ppermute | solution.py:48
  52.8 0.7 %join.1 = bf16[256,512]{1,0:T(8,128)(2,1)} custom-call(bf16[128,384]{1,0:T(8,128)(2,1)S(1)} %adam.3.refs_0_, bf16[128,128]{1,0:T(8,128)(2,1)S(1)} %adam.4.refs_1_, bf16[128,384]{1,0:T(8,128)(2,1)S(1)} %collective-permute-done.20.refs_2_, bf16[128,128]{1,0:T(8,128)(2,1)S(1)} %collective-permute-done.21.refs_3_), custom_call_target="tpu_custom_call" | custom-call | tf_op jit(solution)/shard_map/join/pallas_call | solution.py:218
  (41 shorter events, 3.5 us)
Async XLA Ops:
  0.6 4.6 %copy-start = (bf16[128,512]{1,0:T(8,128)(2,1)S(1)}, bf16[128,512]{1,0:T(8,128)(2,1)}, u32[]{:S(2)}) copy-start(bf16[128,512]{1,0:T(8,128)(2,1)} %refs_0_.18) | copy-start | bytes 393220
  0.6 1.3 %copy-start.4 = (bf16[128,4096]{1,0:T(8,128)(2,1)S(1)}, bf16[128,4096]{1,0:T(8,128)(2,1)}, u32[]{:S(2)}) copy-start(bf16[128,4096]{1,0:T(8,128)(2,1)} %source.1) | copy-start | bytes 3145732
  2.2 8.0 %collective-permute-start.13 = (bf16[128,256]{1,0:T(8,128)(2,1)S(1)}, bf16[128,256]{1,0:T(8,128)(2,1)S(1)}, u32[]{:S(2)}, u32[]{:S(2)}) collective-permute-start(bf16[128,256]{1,0:T(8,128)(2,1)S(1)} %get-tuple-element.26), channel_id=1, source_target_pairs={{0,4},{1,5},{2,6},{3,7},{4,0},{5,1},{6,2},{7,3},{8,12},{9,13},{10,... | collective-permute-start | bytes 196616 | tf_op jit(solution)/shard_map/ppermute | solution.py:48
  5.2 9.4 %collective-permute-start = (bf16[128,512]{1,0:T(8,128)(2,1)S(1)}, bf16[128,512]{1,0:T(8,128)(2,1)S(1)}, u32[]{:S(2)}, u32[]{:S(2)}) collective-permute-start(bf16[128,512]{1,0:T(8,128)(2,1)S(1)} %copy-done), channel_id=1, source_target_pairs={{0,4},{1,5},{2,6},{3,7},{4,0},{5,1},{6,2},{7,3},{8,12},{9,13},{10,... | collective-permute-start | bytes 393224 | tf_op jit(solution)/shard_map/ppermute | solution.py:48
  5.3 5.8 %collective-permute-start.14 = (bf16[128,256]{1,0:T(8,128)(2,1)S(1)}, bf16[128,256]{1,0:T(8,128)(2,1)S(1)}, u32[]{:S(2)}, u32[]{:S(2)}) collective-permute-start(bf16[128,256]{1,0:T(8,128)(2,1)S(1)} %get-tuple-element.27), channel_id=1, source_target_pairs={{0,1},{1,0},{2,3},{3,2},{4,5},{5,4},{6,7},{7,6},{8,9},{9,8},{10,11... | collective-permute-start | bytes 196616 | tf_op jit(solution)/shard_map/ppermute | solution.py:48
  7.2 5.9 %collective-permute-start.15 = (bf16[128,256]{1,0:T(8,128)(2,1)S(1)}, bf16[128,256]{1,0:T(8,128)(2,1)S(1)}, u32[]{:S(2)}, u32[]{:S(2)}) collective-permute-start(bf16[128,256]{1,0:T(8,128)(2,1)S(1)} %get-tuple-element.28), channel_id=1, source_target_pairs={{0,5},{1,4},{2,7},{3,6},{4,1},{5,0},{6,3},{7,2},{8,13},{9,12},{10,... | collective-permute-start | bytes 196616 | tf_op jit(solution)/shard_map/ppermute | solution.py:48
  8.7 7.5 %collective-permute-start.1 = (bf16[128,512]{1,0:T(8,128)(2,1)S(1)}, bf16[128,512]{1,0:T(8,128)(2,1)S(1)}, u32[]{:S(2)}, u32[]{:S(2)}) collective-permute-start(bf16[128,512]{1,0:T(8,128)(2,1)S(1)} %copy-done), channel_id=1, source_target_pairs={{0,1},{1,0},{2,3},{3,2},{4,5},{5,4},{6,7},{7,6},{8,9},{9,8},{10,11... | collective-permute-start | bytes 393224 | tf_op jit(solution)/shard_map/ppermute | solution.py:48
  10.2 8.5 %collective-permute-start.2 = (bf16[128,512]{1,0:T(8,128)(2,1)S(1)}, bf16[128,512]{1,0:T(8,128)(2,1)S(1)}, u32[]{:S(2)}, u32[]{:S(2)}) collective-permute-start(bf16[128,512]{1,0:T(8,128)(2,1)S(1)} %copy-done), channel_id=1, source_target_pairs={{0,5},{1,4},{2,7},{3,6},{4,1},{5,0},{6,3},{7,2},{8,13},{9,12},{10,... | collective-permute-start | bytes 393224 | tf_op jit(solution)/shard_map/ppermute | solution.py:48
  11.1 9.6 %collective-permute-start.7 = (bf16[128,512]{1,0:T(8,128)(2,1)S(1)}, bf16[128,512]{1,0:T(8,128)(2,1)S(1)}, u32[]{:S(2)}, u32[]{:S(2)}) collective-permute-start(bf16[128,512]{1,0:T(8,128)(2,1)S(1)} %get-tuple-element.22), channel_id=1, source_target_pairs={{0,4},{1,5},{2,6},{3,7},{4,0},{5,1},{6,2},{7,3},{8,12},{9,13},{10,... | collective-permute-start | bytes 393224 | tf_op jit(solution)/shard_map/ppermute | solution.py:48
  13.1 8.2 %collective-permute-start.8 = (bf16[128,512]{1,0:T(8,128)(2,1)S(1)}, bf16[128,512]{1,0:T(8,128)(2,1)S(1)}, u32[]{:S(2)}, u32[]{:S(2)}) collective-permute-start(bf16[128,512]{1,0:T(8,128)(2,1)S(1)} %get-tuple-element.23), channel_id=1, source_target_pairs={{0,1},{1,0},{2,3},{3,2},{4,5},{5,4},{6,7},{7,6},{8,9},{9,8},{10,11... | collective-permute-start | bytes 393224 | tf_op jit(solution)/shard_map/ppermute | solution.py:48
  14.7 8.4 %collective-permute-start.9 = (bf16[128,512]{1,0:T(8,128)(2,1)S(1)}, bf16[128,512]{1,0:T(8,128)(2,1)S(1)}, u32[]{:S(2)}, u32[]{:S(2)}) collective-permute-start(bf16[128,512]{1,0:T(8,128)(2,1)S(1)} %get-tuple-element.24), channel_id=1, source_target_pairs={{0,5},{1,4},{2,7},{3,6},{4,1},{5,0},{6,3},{7,2},{8,13},{9,12},{10,... | collective-permute-start | bytes 393224 | tf_op jit(solution)/shard_map/ppermute | solution.py:48
  19.0 8.8 %collective-permute-start.16 = (bf16[128,512]{1,0:T(8,128)(2,1)S(1)}, bf16[128,512]{1,0:T(8,128)(2,1)S(1)}, u32[]{:S(2)}, u32[]{:S(2)}) collective-permute-start(bf16[128,512]{1,0:T(8,128)(2,1)S(1)} %bitcast.19), channel_id=1, source_target_pairs={{0,2},{1,3},{2,0},{3,1},{4,6},{5,7},{6,4},{7,5},{8,10},{9,11},{10,... | collective-permute-start | bytes 393224 | tf_op jit(solution)/shard_map/ppermute | solution.py:48
  19.1 5.3 %collective-permute-start.3 = (bf16[128,256]{1,0:T(8,128)(2,1)S(1)}, bf16[128,256]{1,0:T(8,128)(2,1)S(1)}, u32[]{:S(2)}, u32[]{:S(2)}) collective-permute-start(bf16[128,256]{1,0:T(8,128)(2,1)S(1)} %get-tuple-element.18), channel_id=1, source_target_pairs={{0,4},{1,5},{2,6},{3,7},{4,0},{5,1},{6,2},{7,3},{8,12},{9,13},{10,... | collective-permute-start | bytes 196616 | tf_op jit(solution)/shard_map/ppermute | solution.py:48
  20.8 4.7 %collective-permute-start.4 = (bf16[128,256]{1,0:T(8,128)(2,1)S(1)}, bf16[128,256]{1,0:T(8,128)(2,1)S(1)}, u32[]{:S(2)}, u32[]{:S(2)}) collective-permute-start(bf16[128,256]{1,0:T(8,128)(2,1)S(1)} %get-tuple-element.19), channel_id=1, source_target_pairs={{0,1},{1,0},{2,3},{3,2},{4,5},{5,4},{6,7},{7,6},{8,9},{9,8},{10,11... | collective-permute-start | bytes 196616 | tf_op jit(solution)/shard_map/ppermute | solution.py:48
  21.3 5.2 %collective-permute-start.5 = (bf16[128,256]{1,0:T(8,128)(2,1)S(1)}, bf16[128,256]{1,0:T(8,128)(2,1)S(1)}, u32[]{:S(2)}, u32[]{:S(2)}) collective-permute-start(bf16[128,256]{1,0:T(8,128)(2,1)S(1)} %get-tuple-element.20), channel_id=1, source_target_pairs={{0,5},{1,4},{2,7},{3,6},{4,1},{5,0},{6,3},{7,2},{8,13},{9,12},{10,... | collective-permute-start | bytes 196616 | tf_op jit(solution)/shard_map/ppermute | solution.py:48
  23.4 6.7 %collective-permute-start.12 = (bf16[128,512]{1,0:T(8,128)(2,1)S(1)}, bf16[128,512]{1,0:T(8,128)(2,1)S(1)}, u32[]{:S(2)}, u32[]{:S(2)}) collective-permute-start(bf16[128,512]{1,0:T(8,128)(2,1)S(1)} %bitcast.20), channel_id=1, source_target_pairs={{0,2},{1,3},{2,0},{3,1},{4,6},{5,7},{6,4},{7,5},{8,10},{9,11},{10,... | collective-permute-start | bytes 393224 | tf_op jit(solution)/shard_map/ppermute | solution.py:48
  24.5 5.1 %collective-permute-start.10 = (bf16[128,512]{1,0:T(8,128)(2,1)S(1)}, bf16[128,512]{1,0:T(8,128)(2,1)S(1)}, u32[]{:S(2)}, u32[]{:S(2)}) collective-permute-start(bf16[128,512]{1,0:T(8,128)(2,1)S(1)} %bitcast.22), channel_id=1, source_target_pairs={{0,2},{1,3},{2,0},{3,1},{4,6},{5,7},{6,4},{7,5},{8,10},{9,11},{10,... | collective-permute-start | bytes 393224 | tf_op jit(solution)/shard_map/ppermute | solution.py:48
  26.8 10.6 %collective-permute-start.6 = (bf16[128,512]{1,0:T(8,128)(2,1)S(1)}, bf16[128,512]{1,0:T(8,128)(2,1)S(1)}, u32[]{:S(2)}, u32[]{:S(2)}) collective-permute-start(bf16[128,512]{1,0:T(8,128)(2,1)S(1)} %bitcast.21), channel_id=1, source_target_pairs={{0,2},{1,3},{2,0},{3,1},{4,6},{5,7},{6,4},{7,5},{8,10},{9,11},{10,... | collective-permute-start | bytes 393224 | tf_op jit(solution)/shard_map/ppermute | solution.py:48
  27.9 6.4 %collective-permute-start.17 = (bf16[128,512]{1,0:T(8,128)(2,1)S(1)}, bf16[128,512]{1,0:T(8,128)(2,1)S(1)}, u32[]{:S(2)}, u32[]{:S(2)}) collective-permute-start(bf16[128,512]{1,0:T(8,128)(2,1)S(1)} %fusion), channel_id=1, source_target_pairs={{0,8},{1,9},{2,10},{3,11},{4,12},{5,13},{6,14},{7,15},{8,0},{9,1},... | collective-permute-start | bytes 393224 | tf_op jit(solution)/shard_map/ppermute | solution.py:48
  29.6 7.8 %collective-permute-start.11 = (bf16[128,512]{1,0:T(8,128)(2,1)S(1)}, bf16[128,512]{1,0:T(8,128)(2,1)S(1)}, u32[]{:S(2)}, u32[]{:S(2)}) collective-permute-start(bf16[128,512]{1,0:T(8,128)(2,1)S(1)} %fusion.1), channel_id=1, source_target_pairs={{0,8},{1,9},{2,10},{3,11},{4,12},{5,13},{6,14},{7,15},{8,0},{9,1},... | collective-permute-start | bytes 393224 | tf_op jit(solution)/shard_map/ppermute | solution.py:48
  34.4 7.4 %copy-start.1 = (f32[128,512]{1,0:T(8,128)S(1)}, f32[128,512]{1,0:T(8,128)}, u32[]{:S(2)}) copy-start(f32[128,512]{1,0:T(8,128)} %refs_0_.21) | copy-start | bytes 786436
  34.4 7.3 %copy-start.2 = (f32[128,512]{1,0:T(8,128)S(1)}, f32[128,512]{1,0:T(8,128)}, u32[]{:S(2)}) copy-start(f32[128,512]{1,0:T(8,128)} %refs_1_.5) | copy-start | bytes 786436
  34.4 7.3 %copy-start.3 = (f32[128,512]{1,0:T(8,128)S(1)}, f32[128,512]{1,0:T(8,128)}, u32[]{:S(2)}) copy-start(f32[128,512]{1,0:T(8,128)} %refs_2_.5) | copy-start | bytes 786436
  34.4 7.3 %collective-permute-start.18 = (bf16[128,384]{1,0:T(8,128)(2,1)S(1)}, bf16[128,384]{1,0:T(8,128)(2,1)S(1)}, u32[]{:S(2)}, u32[]{:S(2)}) collective-permute-start(bf16[128,384]{1,0:T(8,128)(2,1)S(1)} %fusion.3), channel_id=1, source_target_pairs={{0,16},{1,17},{2,18},{3,19},{4,20},{5,21},{6,22},{7,23},{8,24},{9,... | collective-permute-start | bytes 294920 | tf_op jit(solution)/shard_map/ppermute | solution.py:48
  42.0 10.8 %collective-permute-start.20 = (bf16[128,384]{1,0:T(8,128)(2,1)S(1)}, bf16[128,384]{1,0:T(8,128)(2,1)S(1)}, u32[]{:S(2)}, u32[]{:S(2)}) collective-permute-start(bf16[128,384]{1,0:T(8,128)(2,1)S(1)} %adam.3.refs_0_), channel_id=1, source_target_pairs={{0,1},{1,0},{2,3},{3,2},{4,5},{5,4},{6,7},{7,6},{8,9},{9,8},{10,11... | collective-permute-start | bytes 294920 | tf_op jit(solution)/shard_map/ppermute | solution.py:48
  43.5 5.2 %collective-permute-start.19 = (bf16[128,128]{1,0:T(8,128)(2,1)S(1)}, bf16[128,128]{1,0:T(8,128)(2,1)S(1)}, u32[]{:S(2)}, u32[]{:S(2)}) collective-permute-start(bf16[128,128]{1,0:T(8,128)(2,1)S(1)} %fusion.5), channel_id=1, source_target_pairs={{0,16},{1,17},{2,18},{3,19},{4,20},{5,21},{6,22},{7,23},{8,24},{9,... | collective-permute-start | bytes 98312 | tf_op jit(solution)/shard_map/ppermute | solution.py:48
  48.8 4.0 %collective-permute-start.21 = (bf16[128,128]{1,0:T(8,128)(2,1)S(1)}, bf16[128,128]{1,0:T(8,128)(2,1)S(1)}, u32[]{:S(2)}, u32[]{:S(2)}) collective-permute-start(bf16[128,128]{1,0:T(8,128)(2,1)S(1)} %adam.4.refs_1_), channel_id=1, source_target_pairs={{0,1},{1,0},{2,3},{3,2},{4,5},{5,4},{6,7},{7,6},{8,9},{9,8},{10,11... | collective-permute-start | bytes 98312 | tf_op jit(solution)/shard_map/ppermute | solution.py:48
